TPU v7x, 32 devices: a whole 2x2x4 slice. The times are simulated.
32 devices in a mesh: ops: 16 (over z, y, x), blk: 2 (over core).
Axes of the slice: x: 2, y: 2, z: 4, core: 2. Of those that a mesh axis runs over, the one named last changes fastest.
Arguments:
- operators_left: bfloat16 [1024, 256, 256], P('ops', None, 'blk'), may hold values from -6 to 6
- operators_right: bfloat16 [1024, 256, 256], P('ops'), may hold values from -0.0007324219 to 0.0007324219
- wavefunction: bfloat16 [256, 3, 256], P('blk', None, 'ops'), may hold values from -6 to 6
- rotation: bfloat16 [256, 128], replicated, may hold values from -0.375 to 0.375
- pair_count: int32 [16], P('ops'), may hold values from 16 to 64, as said below
- next_owner: int32 [1024, 1], P('ops'), may hold values from 0 to 15; in each aligned block of 64 rows (0 to 63, 64 to 127, ...) at most 8 rows name the same one
Outputs:
- sigma: float32 [256, 3, 256], P(('ops', 'blk'))
- renewed: bfloat16 [16, 128, 128, 128], P('ops', None, 'blk')
Inputs may be any that keep to these rules, and one draw needn't show every extreme that they name: Each owner's live pairs fill its first pair_count slots; at least one owner has all 64 slots live. `next_owner`: among the 64 slots of one owner, at most 8 name the same next owner.
All inputs are finite; a program needn't handle non-finite values.
Results may differ from a plain program's by a relative error of at most 0.0073.
Values may be sent and summed in bfloat16 or wider, within the bound.
A program may use at most 128 MiB of HBM per device.

v0:
```python
import jax
import jax.numpy as jnp
from jax import lax
from jax.sharding import PartitionSpec as P


def over_slots(operation, operand, live_count, template):
    slot_total = template.shape[0]
    results = jax.vmap(operation)(operand)
    living = lax.iota(jnp.int32, slot_total) < live_count
    living = living.reshape((slot_total,) + (1,) * (results.ndim - 1))
    return jnp.where(living, results, jnp.zeros_like(results))


def per_device(operators_left, operators_right, wavefunction, rotation, pair_count, next_owner):
    slot_total = operators_left.shape[0]
    left_states = operators_left.shape[1]
    half_cols = operators_left.shape[2]
    right_states = operators_right.shape[1]
    vectors = wavefunction.shape[1]
    new_states = rotation.shape[1]
    live_count = pair_count[0]
    rows_half = lax.all_gather(wavefunction, "ops", axis=2, tiled=True)

    def right_apply(single_right):
        return jnp.einsum(
            "inr,sr->ins", rows_half, single_right, preferred_element_type=jnp.float32
        ).astype(jnp.bfloat16)

    products = over_slots(
        right_apply,
        operators_right,
        live_count,
        jnp.zeros((slot_total, half_cols, vectors, right_states), jnp.bfloat16),
    )
    products = products.reshape(slot_total, half_cols, vectors * right_states)
    own_rows = left_states // (lax.axis_size("ops") * lax.axis_size("blk"))
    sigma_flat = lax.psum_scatter(
        jnp.einsum("pij,pjn->in", operators_left, products, preferred_element_type=jnp.float32),
        ("ops", "blk"),
        scatter_dimension=0,
        tiled=True,
    )
    sigma = sigma_flat.reshape(own_rows, vectors, right_states)
    new_half = new_states // lax.axis_size("blk")
    rot_rows = lax.dynamic_slice_in_dim(rotation, lax.axis_index("blk") * half_cols, half_cols, 0)

    def renew_partial(single_left):
        rotated = jnp.einsum(
            "ik,ij->kj", rotation, single_left, preferred_element_type=jnp.float32
        ).astype(jnp.bfloat16)
        return jnp.dot(rotated, rot_rows, preferred_element_type=jnp.float32)

    partials = over_slots(
        renew_partial,
        operators_left,
        live_count,
        jnp.zeros((slot_total, new_states, new_states), jnp.float32),
    )
    renewed = lax.psum_scatter(partials, "blk", scatter_dimension=1, tiled=True).astype(
        jnp.bfloat16
    )
    owners = lax.axis_size("ops")
    capacity = max(2, 2 * slot_total // owners)
    targets = next_owner[:, 0]
    living = lax.iota(jnp.int32, slot_total) < live_count
    chosen = ((targets[:, None] == lax.iota(jnp.int32, owners)[None, :]) & living[:, None]).astype(
        jnp.int32
    )
    earlier = jnp.cumsum(chosen, axis=0) - chosen
    ranking = jnp.sum(earlier * chosen, axis=1)
    address = targets * capacity + ranking
    placing = (
        (address[None, :] == lax.iota(jnp.int32, owners * capacity)[:, None]) & living[None, :]
    ).astype(jnp.bfloat16)
    flat_blocks = renewed.reshape(slot_total, new_half * new_states)
    outgoing = jnp.dot(placing, flat_blocks, preferred_element_type=jnp.float32).astype(
        jnp.bfloat16
    )
    outgoing = outgoing.reshape(owners * capacity, new_half, new_states)
    incoming = lax.all_to_all(outgoing, "ops", split_axis=0, concat_axis=0, tiled=True)
    return (sigma, incoming[None])


def solution(mesh):
    in_specs = (
        P("ops", None, "blk"),
        P("ops", None, None),
        P("blk", None, "ops"),
        P(),
        P("ops"),
        P("ops", None),
    )
    out_specs = (P(("ops", "blk"), None, None), P("ops", None, "blk", None))
    return jax.shard_map(
        per_device, mesh=mesh, in_specs=in_specs, out_specs=out_specs, check_vma=False
    )
```

profile of v0, /device:TPU:2, one launch (start us, length us, event | category | flops | bytes accessed | tf_op | source)
XLA Modules:
  0.0 253.7 jit_solution(13115652851254906840)
XLA Ops:
  8.0 0.0 copy-start
  8.0 0.0 reduce-scatter.5.cloned.1.call-start
  8.7 0.1 copy-done
  8.8 5.4 %select_bitcast_fusion.1 = f32[64,128,128]{2,1,0:T(8,128)} fusion(bf16[64,256,128]{2,1,0:T(8,128)(2,1)} %param.6, pred[64]{0:T(512)(128)(4,1)S(1)} %iota_compare_fusion.2, bf16[256,128]{1,0:T(8,128)(2,1)S(1)} %copy-done, s32[]{:T(128)S(6)} %select_n.19), kind=kOutput, calls=%fused_computation.4 | convolution fusion | flops 807403520 | bytes 8487428 | tf_op jit(solution)/shard_map/vmap()/dot_general | solution.py:52
  14.3 0.0 copy-start.2
  14.3 0.0 reduce-scatter.5.cloned.1.call-update
  14.3 0.6 copy-done.2
  14.9 0.1 fusion.19
  15.0 0.1 reduce_window_sum.11
  15.1 0.2 select_reduce_fusion
  15.3 12.7 %reduce-scatter.5.cloned.1.call-done = f32[64,64,128]{2,1,0:T(8,128)} async-done(((f32[64,128,128]{2,1,0:T(8,128)}), f32[64,64,128]{2,1,0:T(8,128)}) %reduce-scatter.5.cloned.1.call-update) | async-done | bytes 2097168 | tf_op jit(solution)/shard_map/reduce_scatter | solution.py:60
  27.9 1.8 convert_element_type.21
  29.7 0.9 fusion.7
  30.6 0.0 copy-start.1
  30.7 1.9 copy.20
  32.6 7.0 %all-to-all-start = ((bf16[128,64,128]{2,1,0:T(8,128)(2,1)}), bf16[128,64,128]{2,1,0:T(8,128)(2,1)S(1)}, u32[]{:S(2)}, u32[]{:S(2)}) async-start(bf16[128,64,128]{2,1,0:T(8,128)(2,1)} %bitcast.45), calls=%async_computation.1 | async-start | bytes 4194304 | tf_op jit(solution)/shard_map/all_to_all | solution.py:81
  39.6 0.0 reduce-scatter.7.cloned.1.call-start
  39.6 0.0 copy-done.1
  39.6 69.9 %all_gather.3 = bf16[128,3,256]{0,2,1:T(8,128)(2,1)S(1)} all-gather(bf16[128,3,16]{0,2,1:T(8,128)(2,1)S(1)} %copy-done.1), channel_id=1, replica_groups=mesh['ops'=16,'blk'=2] {'ops'}, dimensions={2}, use_global_device_ids=true | all-gather | bytes 208896 | tf_op jit(solution)/shard_map/all_gather | solution.py:23
  109.5 9.8 %select_bitcast_fusion = bf16[64,128,3,256]{3,1,0,2:T(8,128)(2,1)} fusion(pred[64]{0:T(512)(128)(4,1)S(1)} %iota_compare_fusion.2, bf16[64,256,256]{2,1,0:T(8,128)(2,1)} %param.7, bf16[128,3,256]{0,2,1:T(8,128)(2,1)S(1)} %all_gather.3), kind=kOutput, calls=%fused_computation | convolution fusion | flops 3233808384 | bytes 21168192 | tf_op jit(solution)/shard_map/vmap(inr,sr->ins)/dot_general | solution.py:26
  119.3 16.7 %copy.11 = bf16[64,128,3,256]{1,3,2,0:T(8,128)(2,1)} copy(bf16[64,128,3,256]{3,1,0,2:T(8,128)(2,1)} %select_bitcast_fusion) | data formatting | bytes 25165824 | tf_op jit(solution)/shard_map/jit(_where)/select_n | solution.py:12
  136.0 7.7 %convolution_bitcast_fusion = f32[256,768]{0,1:T(8,128)S(1)} fusion(bf16[64,128,768]{1,2,0:T(8,128)(2,1)} %bitcast.43, bf16[64,256,128]{2,1,0:T(8,128)(2,1)} %param.6), kind=kOutput, calls=%fused_computation.8 | convolution fusion | flops 3221225472 | bytes 17563648 | tf_op jit(solution)/shard_map/pij,pjn->in/dot_general | solution.py:39
  143.6 1.1 copy.17
  144.8 0.0 reduce-scatter.7.cloned.1.call-update
  144.8 98.4 %reduce-scatter.7.cloned.1.call-done = f32[8,768]{1,0:T(8,128)} async-done(((f32[256,768]{1,0:T(8,128)}), f32[8,768]{1,0:T(8,128)}) %reduce-scatter.7.cloned.1.call-update) | async-done | bytes 24592
  243.3 0.9 copy.18
  244.2 0.7 copy.13
  244.9 0.0 all-to-all-done
  244.9 1.3 copy.27
  (2 shorter events, 0.0 us)
Async XLA Ops:
  8.0 0.8 copy-start
  8.0 19.9 %reduce-scatter.5.cloned.1.call-start = ((), (), s32[]{:S(2)}) async-start(), calls=%async_computation.3 | async-start | bytes 6291456 | tf_op jit(solution)/shard_map/reduce_scatter | solution.py:60
  14.3 0.7 copy-start.2
  30.6 9.0 %copy-start.1 = (bf16[128,3,16]{0,2,1:T(8,128)(2,1)S(1)}, bf16[128,3,16]{0,2,1:T(8,128)(2,1)}, u32[]{:S(2)}) copy-start(bf16[128,3,16]{0,2,1:T(8,128)(2,1)} %param.8) | copy-start | bytes 36868
  32.6 212.3 %all-to-all-start = ((bf16[128,64,128]{2,1,0:T(8,128)(2,1)}), bf16[128,64,128]{2,1,0:T(8,128)(2,1)S(1)}, u32[]{:S(2)}, u32[]{:S(2)}) async-start(bf16[128,64,128]{2,1,0:T(8,128)(2,1)} %bitcast.45), calls=%async_computation.1 | async-start | bytes 4194304 | tf_op jit(solution)/shard_map/all_to_all | solution.py:81
  39.6 203.7 %reduce-scatter.7.cloned.1.call-start = ((), (), s32[]{:S(2)}) async-start(), calls=%async_computation.4 | async-start | bytes 811008
Sparse Core Ops, SparseCore 0:
  14.4 13.4 reduce-scatter.4
Sparse Core Ops, SparseCore 1:
  144.9 98.3 reduce-scatter.6
where the time goes:
time: 256 us; the launch traced here: 254 us
  waiting for transfers between devices  111 us (43%)
  blocking collectives  69.9 us (27%)
  matrix products  23.8 us (9%)
  local copies, waits for them, and re-layouts  23.5 us (9%)
  between operations  16.2 us (6%)
  starting transfers between devices  7.08 us (3%)
    unnamed x3, waiting for transfers between devices  98.5 us
    all_gather x1, blocking collectives, per_device(): rows_half = lax.all_gather(wavefunction, 'ops', axis=2, tiled=True)  69.9 us
    select_n x1, local copies, waits for them, and re-layouts, over_slots(): return jnp.where(living, results, jnp.zeros_like(results))  16.7 us
    reduce_scatter x1, waiting for transfers between devices, per_device(): lax.psum_scatter(partials, 'blk', scatter_dimension=1, tiled=True)  12.7 us
    dot_general x1, matrix products, right_apply(): jnp.einsum('inr,sr->ins', rows_half, single_right, preferred_element_type...  9.77 us
    dot_general x1, matrix products, per_device(): jnp.einsum('pij,pjn->in', operators_left, products, preferred_element_typ...  7.68 us
    all_to_all x1, starting transfers between devices, per_device(): lax.all_to_all(outgoing, 'ops', split_axis=0, concat_axis=0, tiled=True)  7 us
    unnamed x11, local copies, waits for them, and re-layouts  6.79 us
  transfers between devices with their start and end apart: 3, of which 2 were waited for; matrix products, arithmetic and copies ran while one was open for 15% of the time, Pallas kernels for 0%

commit v1 on v0

v1 whole, which is shorter than its diff:
```python
import functools

import jax
import jax.numpy as jnp
from jax import lax
from jax.experimental import pallas as pl
from jax.experimental.pallas import tpu as pltpu
from jax.sharding import PartitionSpec as P

MESH = pl.DeviceIdType.MESH
CHUNKS = 4
GROUP = 8


def kernel(
    n_ops,
    n_blk,
    inbox_ref,
    count_ref,
    left_hbm,
    right_hbm,
    wave_ref,
    rot_ref,
    sigma_ref,
    renewed_ref,
    left,
    right,
    rot_turned,
    rot_rows,
    rot_cols,
    w_mine,
    w_send,
    w_recv,
    blocks,
    outbox,
    wave_all,
    wave_full,
    z_group,
    total,
    sig_send,
    sig_recv,
    left_sem,
    right_sem,
    w_ssem,
    w_rsem,
    wave_ssem,
    wave_rsem,
    out_ssem,
    out_rsem,
    own_sem,
    sig_ssem,
    sig_rsem,
):
    ops = lax.axis_index("ops")
    blk = lax.axis_index("blk")
    me = ops * n_blk + blk
    n_all = n_ops * n_blk
    slots, left_states, half = left.shape
    right_states = right.shape[1]
    new_half = w_mine.shape[1]
    vectors = sigma_ref.shape[1]
    capacity = outbox.shape[0] // n_ops
    step = slots // CHUNKS

    def left_copy(c):
        at = pl.ds(c * step, step)
        return pltpu.make_async_copy(left_hbm.at[at], left.at[at], left_sem.at[c])

    def right_copy(c):
        at = pl.ds(c * step, step)
        return pltpu.make_async_copy(right_hbm.at[at], right.at[at], right_sem.at[c])

    for c in range(CHUNKS):
        left_copy(c).start()
    for c in range(CHUNKS):
        right_copy(c).start()

    barrier = pltpu.get_barrier_semaphore()

    def greet(s, carry):
        other = lax.rem(me + s, n_all)
        pl.semaphore_signal(
            barrier,
            inc=1,
            device_id={"ops": lax.div(other, n_blk), "blk": lax.rem(other, n_blk)},
            device_id_type=MESH,
        )
        return carry

    lax.fori_loop(1, n_all, greet, 0)

    def w_copy(c):
        at = pl.ds(c * step, step)
        return pltpu.make_async_remote_copy(
            src_ref=w_send.at[at],
            dst_ref=w_recv.at[at],
            send_sem=w_ssem.at[c],
            recv_sem=w_rsem.at[c],
            device_id={"ops": ops, "blk": 1 - blk},
            device_id_type=MESH,
        )

    def wave_copy(s):
        return pltpu.make_async_remote_copy(
            src_ref=wave_ref,
            dst_ref=wave_all.at[ops],
            send_sem=wave_ssem.at[s],
            recv_sem=wave_rsem.at[s],
            device_id={"ops": lax.rem(ops + s, n_ops), "blk": blk},
            device_id_type=MESH,
        )

    def out_copy(s):
        target = lax.rem(ops + s, n_ops)
        return pltpu.make_async_remote_copy(
            src_ref=outbox.at[pl.ds(target * capacity, capacity)],
            dst_ref=renewed_ref.at[0, pl.ds(ops * capacity, capacity)],
            send_sem=out_ssem.at[s],
            recv_sem=out_rsem.at[s],
            device_id={"ops": target, "blk": blk},
            device_id_type=MESH,
        )

    def sig_copy(s):
        other = lax.rem(me + s, n_all)
        return pltpu.make_async_remote_copy(
            src_ref=sig_send.at[other],
            dst_ref=sig_recv.at[me],
            send_sem=sig_ssem.at[s],
            recv_sem=sig_rsem.at[s],
            device_id={"ops": lax.div(other, n_blk), "blk": lax.rem(other, n_blk)},
            device_id_type=MESH,
        )

    rot_turned[...] = rot_ref[...].T
    rot_cols[pl.ds(0, new_half)] = rot_turned[pl.ds(blk * new_half, new_half)]
    rot_cols[pl.ds(new_half, new_half)] = rot_turned[pl.ds((1 - blk) * new_half, new_half)]
    rot_rows[pl.ds(0, half)] = rot_ref[pl.ds(blk * half, half)]
    rot_rows[pl.ds(half, half)] = rot_ref[pl.ds((1 - blk) * half, half)]

    def rotate(i, carry):
        p = 2 * i
        both = jnp.concatenate([left[p], left[p + 1]], axis=1)
        w = jnp.dot(rot_cols[...], both, preferred_element_type=jnp.float32)
        w = w.astype(jnp.bfloat16)
        w_mine[p] = w[:new_half, :half]
        w_mine[p + 1] = w[:new_half, half:]
        w_send[p] = w[new_half:, :half]
        w_send[p + 1] = w[new_half:, half:]
        return carry

    for c in range(CHUNKS):
        left_copy(c).wait()
        lax.fori_loop(c * step // 2, (c + 1) * step // 2, rotate, 0)
        if c == 0:
            pl.semaphore_wait(barrier, n_all - 1)
        else:
            w_copy(c - 1).start()

    def start_wave(s, carry):
        wave_copy(s).start()
        return carry

    lax.fori_loop(1, n_ops, start_wave, 0)
    wave_all[ops] = wave_ref[...]
    w_copy(CHUNKS - 1).start()

    blocks[slots] = jnp.zeros(blocks.shape[1:], blocks.dtype)
    part = 4

    def renew(i, carry):
        at = pl.ds(i * part, part)
        w = jnp.concatenate(
            [
                w_mine[at].reshape(part * new_half, half),
                w_recv[at].reshape(part * new_half, half),
            ],
            axis=1,
        )
        b = jnp.dot(w, rot_rows[...], preferred_element_type=jnp.float32)
        blocks[at] = b.astype(jnp.bfloat16).reshape(part, new_half, b.shape[1])
        return carry

    for c in range(CHUNKS):
        w_copy(c).wait()
        lax.fori_loop(c * step // part, (c + 1) * step // part, renew, 0)

    def fill(s):
        first = lax.rem(ops + s, n_ops) * capacity
        for a in range(capacity):
            outbox[first + a] = blocks[inbox_ref[first + a]]

    fill(1)

    def fill_and_send(s, carry):
        fill(s + 1)
        out_copy(s).start()
        return carry

    lax.fori_loop(1, n_ops, fill_and_send, 0)

    def wait_wave(s, carry):
        wave_copy(s).wait()
        return carry

    lax.fori_loop(1, n_ops, wait_wave, 0)
    padded = wave_all.shape[1]
    gathered = wave_all[...].reshape(n_ops * padded, wave_all.shape[2])
    columns = right_states // n_ops
    if padded == columns:
        wave_full[...] = gathered
    else:
        row = lax.broadcasted_iota(jnp.int32, (right_states, n_ops * padded), 0)
        col = lax.broadcasted_iota(jnp.int32, (right_states, n_ops * padded), 1)
        pick = (row // columns) * padded + row % columns == col
        wave_full[...] = jnp.dot(
            pick.astype(jnp.bfloat16), gathered, preferred_element_type=jnp.float32
        ).astype(jnp.bfloat16)

    own = pltpu.make_async_copy(
        outbox.at[pl.ds(ops * capacity, capacity)],
        renewed_ref.at[0, pl.ds(ops * capacity, capacity)],
        own_sem,
    )
    own.start()

    total[...] = jnp.zeros_like(total)

    def apply(g, carry):
        for q in range(GROUP):
            p = g * GROUP + q
            scale = jnp.where(p < count_ref[0], 1.0, 0.0).astype(jnp.float32)
            z = jnp.dot(right[p], wave_full[...], preferred_element_type=jnp.float32)
            z = (z * scale).astype(jnp.bfloat16)
            for n in range(vectors):
                z_group[pl.ds(n * right_states, right_states), pl.ds(q * half, half)] = z[
                    :, n * half : (n + 1) * half
                ]
        lefts = jnp.concatenate([left[g * GROUP + q] for q in range(GROUP)], axis=1)
        for n in range(vectors):
            at = pl.ds(n * right_states, right_states)
            total[at] += lax.dot_general(
                z_group[at],
                lefts,
                (((1,), (1,)), ((), ())),
                preferred_element_type=jnp.float32,
            )
        return carry

    for c in range(CHUNKS):
        right_copy(c).wait()
        lax.fori_loop(c * step // GROUP, (c + 1) * step // GROUP, apply, 0)

    rows = sigma_ref.shape[0]
    for n in range(vectors):
        turned = total[pl.ds(n * right_states, right_states)].T
        sig_send[:, :, pl.ds(n * right_states, right_states)] = turned.reshape(
            n_all, rows, right_states
        ).astype(jnp.bfloat16)
    sig_recv[me] = sig_send[me]

    def start_sig(s, carry):
        sig_copy(s).start()
        return carry

    lax.fori_loop(1, n_all, start_sig, 0)

    def wait_sig(s, carry):
        sig_copy(s).wait()
        return carry

    lax.fori_loop(1, n_all, wait_sig, 0)
    summed = jnp.sum(sig_recv[...].astype(jnp.float32), axis=0)
    for n in range(vectors):
        sigma_ref[:, n, :] = summed[:, n * right_states : (n + 1) * right_states]

    def wait_out(s, carry):
        out_copy(s).wait()
        return carry

    lax.fori_loop(1, n_ops, wait_out, 0)
    own.wait()


def per_device(operators_left, operators_right, wavefunction, rotation, pair_count, next_owner):
    n_ops = lax.axis_size("ops")
    n_blk = lax.axis_size("blk")
    slots, left_states, half = operators_left.shape
    right_states = operators_right.shape[1]
    _, vectors, columns = wavefunction.shape
    new_states = rotation.shape[1]
    new_half = new_states // n_blk
    capacity = max(2, 2 * slots // n_ops)
    n_all = n_ops * n_blk
    rows = left_states // n_all

    targets = next_owner[:, 0]
    number = lax.iota(jnp.int32, slots)
    living = number < pair_count[0]
    same = (targets[:, None] == targets[None, :]) & (number[None, :] < number[:, None])
    ranking = jnp.sum((same & living[None, :]).astype(jnp.int32), axis=1)
    address = jnp.where(living, targets * capacity + ranking, -1)
    hit = address[None, :] == lax.iota(jnp.int32, n_ops * capacity)[:, None]
    source = jnp.min(jnp.where(hit, number[None, :], slots), axis=1)

    padded = -(-columns // 16) * 16
    wave = wavefunction.transpose(2, 1, 0).reshape(columns, vectors * half)
    wave = jnp.pad(wave, ((0, padded - columns), (0, 0)))

    bf16 = jnp.bfloat16
    dma = pltpu.SemaphoreType.DMA
    vmem = pl.BlockSpec(memory_space=pltpu.VMEM)
    smem = pl.BlockSpec(memory_space=pltpu.SMEM)
    anywhere = pl.BlockSpec(memory_space=pl.ANY)
    return pl.pallas_call(
        functools.partial(kernel, n_ops, n_blk),
        out_shape=(
            jax.ShapeDtypeStruct((rows, vectors, right_states), jnp.float32),
            jax.ShapeDtypeStruct((1, n_ops * capacity, new_half, new_states), bf16),
        ),
        in_specs=[smem, smem, anywhere, anywhere, vmem, vmem],
        out_specs=(vmem, anywhere),
        scratch_shapes=[
            pltpu.VMEM((slots, left_states, half), bf16),
            pltpu.VMEM((slots, right_states, right_states), bf16),
            pltpu.VMEM((new_states, left_states), bf16),
            pltpu.VMEM((left_states, new_states), bf16),
            pltpu.VMEM((new_states, left_states), bf16),
            pltpu.VMEM((slots, new_half, half), bf16),
            pltpu.VMEM((slots, new_half, half), bf16),
            pltpu.VMEM((slots, new_half, half), bf16),
            pltpu.VMEM((slots + 1, new_half, new_states), bf16),
            pltpu.VMEM((n_ops * capacity, new_half, new_states), bf16),
            pltpu.VMEM((n_ops, padded, vectors * half), bf16),
            pltpu.VMEM((right_states, vectors * half), bf16),
            pltpu.VMEM((vectors * right_states, GROUP * half), bf16),
            pltpu.VMEM((vectors * right_states, left_states), jnp.float32),
            pltpu.VMEM((n_all, rows, vectors * right_states), bf16),
            pltpu.VMEM((n_all, rows, vectors * right_states), bf16),
            dma((CHUNKS,)),
            dma((CHUNKS,)),
            dma((CHUNKS,)),
            dma((CHUNKS,)),
            dma((n_ops,)),
            dma((n_ops,)),
            dma((n_ops,)),
            dma((n_ops,)),
            dma(()),
            dma((n_all,)),
            dma((n_all,)),
        ],
        compiler_params=pltpu.CompilerParams(collective_id=0, has_side_effects=True),
        name="davidson_step",
    )(source, pair_count, operators_left, operators_right, wave, rotation)


def solution(mesh):
    in_specs = (
        P("ops", None, "blk"),
        P("ops", None, None),
        P("blk", None, "ops"),
        P(),
        P("ops"),
        P("ops", None),
    )
    out_specs = (P(("ops", "blk"), None, None), P("ops", None, "blk", None))
    return jax.shard_map(
        per_device, mesh=mesh, in_specs=in_specs, out_specs=out_specs, check_vma=False
    )
```

time: 256 us -> 83.6 us (0.33)
  the two profiles are of different devices: /device:TPU:2 before, /device:TPU:0 now
where the time goes in v1:
time: 83.6 us; the launch traced here: 83.3 us
  Pallas kernels  74.7 us (89%)
  local copies, waits for them, and re-layouts  5.06 us (6%)
  other arithmetic  2.2 us (3%)
  between operations  1.32 us (2%)
    pallas_call x1, Pallas kernels, per_device(): pl.pallas_call(functools.partial(kernel, n_ops, n_blk), out_shape=(jax.Sh...  74.7 us
    unnamed x3, local copies, waits for them, and re-layouts  3.09 us

profile of v1, /device:TPU:0, one launch (start us, length us, event | category | flops | bytes accessed | tf_op | source)
XLA Modules:
  0.0 83.3 jit_solution(8839795321462011081)
XLA Ops:
  0.6 0.0 copy-start
  1.3 0.9 %convert_reduce_fusion = s32[64]{0:T(128)S(1)} fusion(s32[64]{0:T(128)} %bitcast.11, pred[64]{0:T(512)(128)(4,1)S(1)} %iota_compare_fusion.2), kind=kLoop, calls=%fused_computation.2 | loop fusion | flops 24512 | bytes 576 | tf_op jit(solution)/shard_map/reduce_sum | solution.py:301
  2.2 0.7 add_select_fusion
  2.9 0.6 select_reduce_fusion.inbox_ref
  3.5 0.0 copy-done
  3.5 0.6 copy_bitcast_fusion.wave_ref
  4.1 74.7 %davidson_step.1 = (f32[8,3,256]{2,1,0:T(4,128)}, bf16[1,128,64,128]{3,2,1,0:T(8,128)(2,1)}) custom-call(s32[128]{0:T(128)} %select_reduce_fusion.inbox_ref, s32[1]{0:T(128)} %copy.17.count_ref, bf16[64,256,128]{2,1,0:T(8,128)(2,1)} %left_hbm.1, bf16[64,256,256]{2,1,0:T(8,128)(2,1)} %right_hbm.1, bf16[16,384]{1,0:T(8,128)(2,1)} %copy_bitcast_fusion.wave_ref, ...), custom_call_target="tpu_custom_call" | custom-call | tf_op jit(solution)/shard_map/davidson_step/pallas_call | solution.py:315
  78.8 1.4 %copy.13 = f32[8,3,256]{2,0,1:T(8,128)} copy(f32[8,3,256]{2,1,0:T(4,128)} %get-tuple-element.6) | data formatting | bytes 49152 | tf_op jit(solution)/shard_map/davidson_step/pallas_call | solution.py:315
  80.2 3.1 %copy.18 = bf16[1,128,64,128]{3,2,1,0:T(8,128)(2,1)} copy(bf16[1,128,64,128]{3,2,1,0:T(8,128)(2,1)} %get-tuple-element.11) | data formatting | bytes 4194304
  (1 shorter events, 0.0 us)
Async XLA Ops:
  0.6 2.9 %copy-start = (bf16[128,3,16]{0,2,1:T(8,128)(2,1)S(1)}, bf16[128,3,16]{0,2,1:T(8,128)(2,1)}, u32[]{:S(2)}) copy-start(bf16[128,3,16]{0,2,1:T(8,128)(2,1)} %param.8) | copy-start | bytes 36868

commit v2 on v1

--- a/solution.py
+++ b/solution.py
@@ -39,6 +39,8 @@
     total,
     sig_send,
     sig_recv,
+    mid_send,
+    mid_recv,
     left_sem,
     right_sem,
     w_ssem,
@@ -50,6 +52,8 @@
     own_sem,
     sig_ssem,
     sig_rsem,
+    mid_ssem,
+    mid_rsem,
 ):
     ops = lax.axis_index("ops")
     blk = lax.axis_index("blk")
@@ -72,9 +76,6 @@
 
     for c in range(CHUNKS):
         left_copy(c).start()
-    for c in range(CHUNKS):
-        right_copy(c).start()
-
     barrier = pltpu.get_barrier_semaphore()
 
     def greet(s, carry):
@@ -110,8 +111,14 @@
             device_id_type=MESH,
         )
 
+    near = n_ops // 2
+
+    def out_target(s):
+        side = lax.rem(lax.div(ops, near) + s // near, 2)
+        return side * near + lax.rem(lax.rem(ops, near) + s % near, near)
+
     def out_copy(s):
-        target = lax.rem(ops + s, n_ops)
+        target = out_target(s)
         return pltpu.make_async_remote_copy(
             src_ref=outbox.at[pl.ds(target * capacity, capacity)],
             dst_ref=renewed_ref.at[0, pl.ds(ops * capacity, capacity)],
@@ -121,14 +128,31 @@
             device_id_type=MESH,
         )
 
+    inner = sig_recv.shape[0]
+    layer, place = lax.div(me, inner), lax.rem(me, inner)
+    outer = sig_recv.shape[1]
+
     def sig_copy(s):
-        other = lax.rem(me + s, n_all)
+        other = lax.rem(place + s, inner)
+        device = layer * inner + other
         return pltpu.make_async_remote_copy(
             src_ref=sig_send.at[other],
-            dst_ref=sig_recv.at[me],
+            dst_ref=sig_recv.at[place],
             send_sem=sig_ssem.at[s],
             recv_sem=sig_rsem.at[s],
-            device_id={"ops": lax.div(other, n_blk), "blk": lax.rem(other, n_blk)},
+            device_id={"ops": lax.div(device, n_blk), "blk": lax.rem(device, n_blk)},
+            device_id_type=MESH,
+        )
+
+    def mid_copy(s):
+        other = lax.rem(layer + s, outer)
+        device = other * inner + place
+        return pltpu.make_async_remote_copy(
+            src_ref=mid_send.at[other],
+            dst_ref=mid_recv.at[layer],
+            send_sem=mid_ssem.at[s],
+            recv_sem=mid_rsem.at[s],
+            device_id={"ops": lax.div(device, n_blk), "blk": lax.rem(device, n_blk)},
             device_id_type=MESH,
         )
 
@@ -157,6 +181,9 @@
         else:
             w_copy(c - 1).start()
 
+    for c in range(CHUNKS):
+        right_copy(c).start()
+
     def start_wave(s, carry):
         wave_copy(s).start()
         return carry
@@ -186,18 +213,27 @@
         lax.fori_loop(c * step // part, (c + 1) * step // part, renew, 0)
 
     def fill(s):
-        first = lax.rem(ops + s, n_ops) * capacity
+        first = out_target(s) * capacity
         for a in range(capacity):
             outbox[first + a] = blocks[inbox_ref[first + a]]
 
-    fill(1)
+    last = n_ops - 1
+    held = n_ops // 8
+    fill(near)
 
     def fill_and_send(s, carry):
         fill(s + 1)
         out_copy(s).start()
         return carry
 
-    lax.fori_loop(1, n_ops, fill_and_send, 0)
+    lax.fori_loop(near, last - held, fill_and_send, 0)
+
+    def fill_rest(s, carry):
+        fill(s)
+        return carry
+
+    lax.fori_loop(last - held + 1, n_ops, fill_rest, 0)
+    lax.fori_loop(0, near, fill_rest, 0)
 
     def wait_wave(s, carry):
         wave_copy(s).wait()
@@ -253,24 +289,44 @@
 
     rows = sigma_ref.shape[0]
     for n in range(vectors):
-        turned = total[pl.ds(n * right_states, right_states)].T
-        sig_send[:, :, pl.ds(n * right_states, right_states)] = turned.reshape(
-            n_all, rows, right_states
-        ).astype(jnp.bfloat16)
-    sig_recv[me] = sig_send[me]
+        at = pl.ds(n * right_states, right_states)
+        turned = total[at].T.reshape(outer, inner, rows, right_states).astype(jnp.bfloat16)
+        for z in range(outer):
+            sig_send[:, z, :, at] = turned[z]
+    sig_recv[place] = sig_send[place]
 
     def start_sig(s, carry):
         sig_copy(s).start()
         return carry
 
-    lax.fori_loop(1, n_all, start_sig, 0)
-
     def wait_sig(s, carry):
         sig_copy(s).wait()
         return carry
 
-    lax.fori_loop(1, n_all, wait_sig, 0)
-    summed = jnp.sum(sig_recv[...].astype(jnp.float32), axis=0)
+    lax.fori_loop(1, inner, start_sig, 0)
+    lax.fori_loop(1, inner, wait_sig, 0)
+    mid_send[...] = jnp.sum(sig_recv[...].astype(jnp.float32), axis=0).astype(jnp.bfloat16)
+    mid_recv[layer] = mid_send[layer]
+
+    def start_mid(s, carry):
+        mid_copy(s).start()
+        return carry
+
+    def wait_mid(s, carry):
+        mid_copy(s).wait()
+        return carry
+
+    lax.fori_loop(1, outer, start_mid, 0)
+
+    def start_out(s, carry):
+        out_copy(s).start()
+        return carry
+
+    lax.fori_loop(last - held, n_ops, start_out, 0)
+    lax.fori_loop(1, near, start_out, 0)
+
+    lax.fori_loop(1, outer, wait_mid, 0)
+    summed = jnp.sum(mid_recv[...].astype(jnp.float32), axis=0)
     for n in range(vectors):
         sigma_ref[:, n, :] = summed[:, n * right_states : (n + 1) * right_states]
 
@@ -293,6 +349,9 @@
     capacity = max(2, 2 * slots // n_ops)
     n_all = n_ops * n_blk
     rows = left_states // n_all
+    inner = n_blk
+    while inner * inner < n_all and n_all % (2 * inner) == 0:
+        inner *= 2
 
     targets = next_owner[:, 0]
     number = lax.iota(jnp.int32, slots)
@@ -335,8 +394,10 @@
             pltpu.VMEM((right_states, vectors * half), bf16),
             pltpu.VMEM((vectors * right_states, GROUP * half), bf16),
             pltpu.VMEM((vectors * right_states, left_states), jnp.float32),
-            pltpu.VMEM((n_all, rows, vectors * right_states), bf16),
-            pltpu.VMEM((n_all, rows, vectors * right_states), bf16),
+            pltpu.VMEM((inner, n_all // inner, rows, vectors * right_states), bf16),
+            pltpu.VMEM((inner, n_all // inner, rows, vectors * right_states), bf16),
+            pltpu.VMEM((n_all // inner, rows, vectors * right_states), bf16),
+            pltpu.VMEM((n_all // inner, rows, vectors * right_states), bf16),
             dma((CHUNKS,)),
             dma((CHUNKS,)),
             dma((CHUNKS,)),
@@ -346,8 +407,10 @@
             dma((n_ops,)),
             dma((n_ops,)),
             dma(()),
-            dma((n_all,)),
-            dma((n_all,)),
+            dma((inner,)),
+            dma((inner,)),
+            dma((n_all // inner,)),
+            dma((n_all // inner,)),
         ],
         compiler_params=pltpu.CompilerParams(collective_id=0, has_side_effects=True),
         name="davidson_step",

time: 83.6 us -> 83.7 us (level)
  the two profiles are of different devices: /device:TPU:0 before, /device:TPU:22 now
where the time goes in v2:
time: 83.7 us; the launch traced here: 83.3 us
  Pallas kernels  74.8 us (89%)
  local copies, waits for them, and re-layouts  5.06 us (6%)
  other arithmetic  2.2 us (3%)
  between operations  1.32 us (2%)
    pallas_call x1, Pallas kernels, per_device(): pl.pallas_call(functools.partial(kernel, n_ops, n_blk), out_shape=(jax.Sh...  74.8 us
    unnamed x3, local copies, waits for them, and re-layouts  3.09 us

profile of v2, /device:TPU:22, one launch (start us, length us, event | category | flops | bytes accessed | tf_op | source)
XLA Modules:
  0.0 83.3 jit_solution(8577382944277082796)
XLA Ops:
  0.6 0.0 copy-start
  1.3 0.9 %convert_reduce_fusion = s32[64]{0:T(128)S(1)} fusion(s32[64]{0:T(128)} %bitcast.11, pred[64]{0:T(512)(128)(4,1)S(1)} %iota_compare_fusion.2), kind=kLoop, calls=%fused_computation.2 | loop fusion | flops 24512 | bytes 576 | tf_op jit(solution)/shard_map/reduce_sum | solution.py:360
  2.2 0.7 add_select_fusion
  2.9 0.6 select_reduce_fusion.inbox_ref
  3.5 0.0 copy-done
  3.5 0.6 copy_bitcast_fusion.wave_ref
  4.1 74.8 %davidson_step.1 = (f32[8,3,256]{2,1,0:T(4,128)}, bf16[1,128,64,128]{3,2,1,0:T(8,128)(2,1)}) custom-call(s32[128]{0:T(128)} %select_reduce_fusion.inbox_ref, s32[1]{0:T(128)} %copy.17.count_ref, bf16[64,256,128]{2,1,0:T(8,128)(2,1)} %left_hbm.1, bf16[64,256,256]{2,1,0:T(8,128)(2,1)} %right_hbm.1, bf16[16,384]{1,0:T(8,128)(2,1)} %copy_bitcast_fusion.wave_ref, ...), custom_call_target="tpu_custom_call" | custom-call | tf_op jit(solution)/shard_map/davidson_step/pallas_call | solution.py:374
  78.9 1.4 %copy.13 = f32[8,3,256]{2,0,1:T(8,128)} copy(f32[8,3,256]{2,1,0:T(4,128)} %get-tuple-element.6) | data formatting | bytes 49152 | tf_op jit(solution)/shard_map/davidson_step/pallas_call | solution.py:374
  80.3 3.1 %copy.18 = bf16[1,128,64,128]{3,2,1,0:T(8,128)(2,1)} copy(bf16[1,128,64,128]{3,2,1,0:T(8,128)(2,1)} %get-tuple-element.11) | data formatting | bytes 4194304
  (1 shorter events, 0.0 us)
Async XLA Ops:
  0.6 2.9 %copy-start = (bf16[128,3,16]{0,2,1:T(8,128)(2,1)S(1)}, bf16[128,3,16]{0,2,1:T(8,128)(2,1)}, u32[]{:S(2)}) copy-start(bf16[128,3,16]{0,2,1:T(8,128)(2,1)} %param.8) | copy-start | bytes 36868

commit v3 on v2

--- a/solution.py
+++ b/solution.py
@@ -62,7 +62,7 @@
     slots, left_states, half = left.shape
     right_states = right.shape[1]
     new_half = w_mine.shape[1]
-    vectors = sigma_ref.shape[1]
+    vectors = sigma_ref.shape[0]
     capacity = outbox.shape[0] // n_ops
     step = slots // CHUNKS
 
@@ -163,19 +163,21 @@
     rot_rows[pl.ds(half, half)] = rot_ref[pl.ds((1 - blk) * half, half)]
 
     def rotate(i, carry):
-        p = 2 * i
-        both = jnp.concatenate([left[p], left[p + 1]], axis=1)
-        w = jnp.dot(rot_cols[...], both, preferred_element_type=jnp.float32)
-        w = w.astype(jnp.bfloat16)
-        w_mine[p] = w[:new_half, :half]
-        w_mine[p + 1] = w[:new_half, half:]
-        w_send[p] = w[new_half:, :half]
-        w_send[p + 1] = w[new_half:, half:]
+        turned = rot_cols[...]
+        for q in range(0, GROUP, 2):
+            p = GROUP * i + q
+            both = jnp.concatenate([left[p], left[p + 1]], axis=1)
+            w = jnp.dot(turned, both, preferred_element_type=jnp.float32)
+            w = w.astype(jnp.bfloat16)
+            w_mine[p] = w[:new_half, :half]
+            w_mine[p + 1] = w[:new_half, half:]
+            w_send[p] = w[new_half:, :half]
+            w_send[p + 1] = w[new_half:, half:]
         return carry
 
     for c in range(CHUNKS):
         left_copy(c).wait()
-        lax.fori_loop(c * step // 2, (c + 1) * step // 2, rotate, 0)
+        lax.fori_loop(c * step // GROUP, (c + 1) * step // GROUP, rotate, 0)
         if c == 0:
             pl.semaphore_wait(barrier, n_all - 1)
         else:
@@ -193,7 +195,7 @@
     w_copy(CHUNKS - 1).start()
 
     blocks[slots] = jnp.zeros(blocks.shape[1:], blocks.dtype)
-    part = 4
+    part = step
 
     def renew(i, carry):
         at = pl.ds(i * part, part)
@@ -217,23 +219,19 @@
         for a in range(capacity):
             outbox[first + a] = blocks[inbox_ref[first + a]]
 
-    last = n_ops - 1
-    held = n_ops // 8
+    def turn(t):
+        return 1 + lax.rem(t + near - 1, n_ops - 1)
+
     fill(near)
 
-    def fill_and_send(s, carry):
-        fill(s + 1)
-        out_copy(s).start()
-        return carry
-
-    lax.fori_loop(near, last - held, fill_and_send, 0)
-
-    def fill_rest(s, carry):
-        fill(s)
-        return carry
-
-    lax.fori_loop(last - held + 1, n_ops, fill_rest, 0)
-    lax.fori_loop(0, near, fill_rest, 0)
+    def fill_and_send(t, carry):
+        fill(turn(t + 1))
+        out_copy(turn(t)).start()
+        return carry
+
+    lax.fori_loop(0, n_ops - 2, fill_and_send, 0)
+    fill(0)
+    out_copy(near - 1).start()
 
     def wait_wave(s, carry):
         wave_copy(s).wait()
@@ -287,7 +285,7 @@
         right_copy(c).wait()
         lax.fori_loop(c * step // GROUP, (c + 1) * step // GROUP, apply, 0)
 
-    rows = sigma_ref.shape[0]
+    rows = sigma_ref.shape[1]
     for n in range(vectors):
         at = pl.ds(n * right_states, right_states)
         turned = total[at].T.reshape(outer, inner, rows, right_states).astype(jnp.bfloat16)
@@ -318,17 +316,10 @@
 
     lax.fori_loop(1, outer, start_mid, 0)
 
-    def start_out(s, carry):
-        out_copy(s).start()
-        return carry
-
-    lax.fori_loop(last - held, n_ops, start_out, 0)
-    lax.fori_loop(1, near, start_out, 0)
-
     lax.fori_loop(1, outer, wait_mid, 0)
     summed = jnp.sum(mid_recv[...].astype(jnp.float32), axis=0)
     for n in range(vectors):
-        sigma_ref[:, n, :] = summed[:, n * right_states : (n + 1) * right_states]
+        sigma_ref[n] = summed[:, n * right_states : (n + 1) * right_states]
 
     def wait_out(s, carry):
         out_copy(s).wait()
@@ -371,10 +362,10 @@
     vmem = pl.BlockSpec(memory_space=pltpu.VMEM)
     smem = pl.BlockSpec(memory_space=pltpu.SMEM)
     anywhere = pl.BlockSpec(memory_space=pl.ANY)
-    return pl.pallas_call(
+    sigma, renewed = pl.pallas_call(
         functools.partial(kernel, n_ops, n_blk),
         out_shape=(
-            jax.ShapeDtypeStruct((rows, vectors, right_states), jnp.float32),
+            jax.ShapeDtypeStruct((vectors, rows, right_states), jnp.float32),
             jax.ShapeDtypeStruct((1, n_ops * capacity, new_half, new_states), bf16),
         ),
         in_specs=[smem, smem, anywhere, anywhere, vmem, vmem],
@@ -415,6 +406,7 @@
         compiler_params=pltpu.CompilerParams(collective_id=0, has_side_effects=True),
         name="davidson_step",
     )(source, pair_count, operators_left, operators_right, wave, rotation)
+    return sigma.transpose(1, 0, 2), renewed
 
 
 def solution(mesh):

time: 83.7 us -> 75.3 us (0.90)
  the two profiles are of different devices: /device:TPU:22 before, /device:TPU:2 now
where the time goes in v3:
time: 75.3 us; the launch traced here: 75 us
  Pallas kernels  66.4 us (88%)
  local copies, waits for them, and re-layouts  5.04 us (7%)
  other arithmetic  2.2 us (3%)
  between operations  1.32 us (2%)
    pallas_call x1, Pallas kernels, per_device(): pl.pallas_call(functools.partial(kernel, n_ops, n_blk), out_shape=(jax.Sh...  66.4 us
    unnamed x4, local copies, waits for them, and re-layouts  4.44 us

profile of v3, /device:TPU:2, one launch (start us, length us, event | category | flops | bytes accessed | tf_op | source)
XLA Modules:
  0.0 75.0 jit_solution(14285952948436687063)
XLA Ops:
  0.6 0.0 copy-start
  1.3 0.9 %convert_reduce_fusion = s32[64]{0:T(128)S(1)} fusion(s32[64]{0:T(128)} %bitcast.13, pred[64]{0:T(512)(128)(4,1)S(1)} %iota_compare_fusion.2), kind=kLoop, calls=%fused_computation.2 | loop fusion | flops 24512 | bytes 576 | tf_op jit(solution)/shard_map/reduce_sum | solution.py:351
  2.2 0.7 add_select_fusion
  2.9 0.6 select_reduce_fusion.inbox_ref
  3.5 0.0 copy-done
  3.5 0.6 copy_bitcast_fusion.wave_ref
  4.1 66.4 %davidson_step.1 = (f32[3,8,256]{2,1,0:T(8,128)}, bf16[1,128,64,128]{3,2,1,0:T(8,128)(2,1)}) custom-call(s32[128]{0:T(128)} %select_reduce_fusion.inbox_ref, s32[1]{0:T(128)} %copy.15.count_ref, bf16[64,256,128]{2,1,0:T(8,128)(2,1)} %left_hbm.1, bf16[64,256,256]{2,1,0:T(8,128)(2,1)} %right_hbm.1, bf16[16,384]{1,0:T(8,128)(2,1)} %copy_bitcast_fusion.wave_ref, ...), custom_call_target="tpu_custom_call" | custom-call | tf_op jit(solution)/shard_map/davidson_step/pallas_call | solution.py:365
  70.6 1.3 %copy.16 = f32[8,3,256]{2,0,1:T(8,128)} copy(f32[8,3,256]{2,0,1:T(8,128)} %bitcast.12) | data formatting | bytes 49152
  71.9 3.1 %copy.17 = bf16[1,128,64,128]{3,2,1,0:T(8,128)(2,1)} copy(bf16[1,128,64,128]{3,2,1,0:T(8,128)(2,1)} %get-tuple-element.9) | data formatting | bytes 4194304
  (1 shorter events, 0.0 us)
Async XLA Ops:
  0.6 2.9 %copy-start = (bf16[128,3,16]{0,2,1:T(8,128)(2,1)S(1)}, bf16[128,3,16]{0,2,1:T(8,128)(2,1)}, u32[]{:S(2)}) copy-start(bf16[128,3,16]{0,2,1:T(8,128)(2,1)} %param.8) | copy-start | bytes 36868

commit v4 on v3

--- a/solution.py
+++ b/solution.py
@@ -366,10 +366,10 @@
         functools.partial(kernel, n_ops, n_blk),
         out_shape=(
             jax.ShapeDtypeStruct((vectors, rows, right_states), jnp.float32),
-            jax.ShapeDtypeStruct((1, n_ops * capacity, new_half, new_states), bf16),
+            pltpu.VMEM((1, n_ops * capacity, new_half, new_states), bf16),
         ),
         in_specs=[smem, smem, anywhere, anywhere, vmem, vmem],
-        out_specs=(vmem, anywhere),
+        out_specs=(vmem, vmem),
         scratch_shapes=[
             pltpu.VMEM((slots, left_states, half), bf16),
             pltpu.VMEM((slots, right_states, right_states), bf16),

time: 75.3 us -> 72.6 us (0.964)
  local copies, waits for them, and re-layouts: 5.04 us -> 2.54 us
    unnamed x4 -> x6, local copies, waits for them, and re-layouts: 4.44 us -> 1.94 us
where the time goes in v4:
time: 72.6 us; the launch traced here: 72.4 us
  Pallas kernels  66.3 us (91%)
  local copies, waits for them, and re-layouts  2.54 us (3%)
  other arithmetic  2.21 us (3%)
  between operations  1.33 us (2%)
    pallas_call x1, Pallas kernels, per_device(): pl.pallas_call(functools.partial(kernel, n_ops, n_blk), out_shape=(jax.Sh...  66.3 us
    unnamed x6, local copies, waits for them, and re-layouts  1.94 us

profile of v4, /device:TPU:2, one launch (start us, length us, event | category | flops | bytes accessed | tf_op | source)
XLA Modules:
  0.0 72.4 jit_solution(2961327310430487902)
XLA Ops:
  0.6 0.0 copy-start
  1.3 0.9 %convert_reduce_fusion = s32[64]{0:T(128)S(1)} fusion(s32[64]{0:T(128)} %bitcast.13, pred[64]{0:T(512)(128)(4,1)S(1)} %iota_compare_fusion.2), kind=kLoop, calls=%fused_computation.2 | loop fusion | flops 24512 | bytes 576 | tf_op jit(solution)/shard_map/reduce_sum | solution.py:351
  2.2 0.7 add_select_fusion
  2.9 0.6 select_reduce_fusion.inbox_ref
  3.5 0.0 copy-done
  3.5 0.6 copy_bitcast_fusion.wave_ref
  4.1 66.3 %davidson_step.1 = (f32[3,8,256]{2,1,0:T(8,128)}, bf16[1,128,64,128]{3,2,1,0:T(8,128)(2,1)S(1)}) custom-call(s32[128]{0:T(128)} %select_reduce_fusion.inbox_ref, s32[1]{0:T(128)} %copy.16.count_ref, bf16[64,256,128]{2,1,0:T(8,128)(2,1)} %left_hbm.1, bf16[64,256,256]{2,1,0:T(8,128)(2,1)} %right_hbm.1, bf16[16,384]{1,0:T(8,128)(2,1)} %copy_bitcast_fusion.wave_ref, ...), custom_call_target="tpu_custom_call" | custom-call | tf_op jit(solution)/shard_map/davidson_step/pallas_call | solution.py:365
  70.5 0.0 copy-start.1
  70.5 1.3 %copy.15 = bf16[1,128,64,128]{3,2,1,0:T(8,128)(2,1)} copy(bf16[1,128,64,128]{3,2,1,0:T(8,128)(2,1)S(1)} %get-tuple-element.7) | data formatting | bytes 4194304
  71.8 0.0 copy-done.1
  71.8 0.6 copy.17
  (1 shorter events, 0.0 us)
Async XLA Ops:
  0.6 2.9 %copy-start = (bf16[128,3,16]{0,2,1:T(8,128)(2,1)S(1)}, bf16[128,3,16]{0,2,1:T(8,128)(2,1)}, u32[]{:S(2)}) copy-start(bf16[128,3,16]{0,2,1:T(8,128)(2,1)} %param.8) | copy-start | bytes 36868
  70.5 1.3 %copy-start.1 = (f32[3,8,256]{2,1,0:T(8,128)S(1)}, f32[3,8,256]{2,1,0:T(8,128)}, u32[]{:S(2)}) copy-start(f32[3,8,256]{2,1,0:T(8,128)} %get-tuple-element.4) | copy-start | bytes 73732
